TPU v7x, 32 devices: a whole 2x2x4 slice. The times are simulated.
32 devices in a mesh: seq: 4 (over z), head: 8 (over y, x, core).
Axes of the slice: x: 2, y: 2, z: 4, core: 2. Of those that a mesh axis runs over, the one named last changes fastest.
Arguments:
- query: float32 [3072, 1024], P('seq', 'head'), may hold values from -6 to 6
- key_in: float32 [3072, 1024], P('seq', 'head'), may hold values from -6 to 6
- value: float32 [3072, 1024], P('seq', 'head'), may hold values from -6 to 6
- out_grad: float32 [3072, 1024], P('seq', 'head'), may hold values from -6 to 6
- head_scale: float32 [8], P('head'), may hold values from 0.5 to 2
- norm_gain: float32 [1024], P('head'), may hold values from 0.5 to 1.5
- group_counts: int32 [4], replicated, may hold values from 1 to 6, 12 in all
Outputs:
- normed: float32 [3072, 1024], P('seq', 'head')
- grad_query: float32 [3072, 1024], P('seq', 'head')
- grad_key: float32 [3072, 1024], P('seq', 'head')
- grad_value: float32 [3072, 1024], P('seq', 'head')
Inputs may be any that keep to these rules, and one draw needn't show every extreme that they name: The live rows of shard i are its first 128 * group_counts[i] rows; the counts sum to 3 * 4 and the largest is exactly 6.
All inputs are finite; a program needn't handle non-finite values.
Results may differ from a plain program's by a relative error of at most 0.0001.
Values sent between devices are 32-bit elements; how exact they have to be, the bound alone decides.
A program may use at most 64 MiB of HBM per device.

v0:
```python
import jax
import jax.numpy as jnp
from jax import lax
from jax.sharding import PartitionSpec as P

GROUP = 128


def plain_product(left, right):
    return jnp.dot(left, right, precision=lax.Precision.HIGHEST, preferred_element_type=jnp.float32)


def leading_product(left, right):
    return lax.dot_general(
        left,
        right,
        (((0,), (0,)), ((), ())),
        precision=lax.Precision.HIGHEST,
        preferred_element_type=jnp.float32,
    )


def on_device(query, key_in, value, out_grad, head_scale, norm_gain, group_counts):
    capacity, features_dev = query.shape
    shard_pos = lax.axis_index("seq")
    block_live = group_counts[shard_pos]
    live_rows = (jnp.arange(capacity) < block_live * GROUP)[:, None]
    q_rows = jnp.where(live_rows, query, 0.0)
    k_rows = jnp.where(live_rows, key_in, 0.0)
    v_rows = jnp.where(live_rows, value, 0.0)
    causal = jnp.tril(jnp.ones((GROUP, GROUP), dtype=bool))
    block_total = capacity // GROUP
    zero_state = jnp.zeros((features_dev, features_dev), jnp.float32)

    def forward_step(block_idx, state_pack):
        running, outputs, saved_states, saved_scores = state_pack
        row_start = block_idx * GROUP
        q_block = lax.dynamic_slice_in_dim(q_rows, row_start, GROUP, 0)
        k_block = lax.dynamic_slice_in_dim(k_rows, row_start, GROUP, 0)
        v_block = lax.dynamic_slice_in_dim(v_rows, row_start, GROUP, 0)
        scores = jnp.where(causal, plain_product(q_block, k_block.T), 0.0)
        local_part = plain_product(q_block, running) + plain_product(scores, v_block)
        outputs = lax.dynamic_update_slice_in_dim(outputs, local_part, row_start, 0)
        saved_states = lax.dynamic_update_index_in_dim(saved_states, running, block_idx, 0)
        saved_scores = lax.dynamic_update_index_in_dim(saved_scores, scores, block_idx, 0)
        running = running + leading_product(k_block, v_block)
        return (running, outputs, saved_states, saved_scores)

    forward_init = (
        zero_state,
        jnp.zeros((capacity, features_dev), jnp.float32),
        jnp.zeros((block_total, features_dev, features_dev), jnp.float32),
        jnp.zeros((block_total, GROUP, GROUP), jnp.float32),
    )
    shard_state, local_out, saved_states, saved_scores = lax.fori_loop(
        0, block_live, forward_step, forward_init
    )
    piece_rows = lax.all_gather(shard_state[None], "seq", axis=0, tiled=True)
    picked = (jnp.arange(piece_rows.shape[0]) < shard_pos)[:, None, None]
    state_in = jnp.sum(jnp.where(picked, piece_rows, 0.0), axis=0)
    attended = local_out + plain_product(q_rows, state_in)
    scaled = attended * head_scale[0]
    features = features_dev * lax.axis_size("head")
    squares, cross_terms = lax.psum(
        (jnp.sum(scaled * scaled, axis=1), jnp.sum(norm_gain[None, :] * out_grad * scaled, axis=1)),
        "head",
    )
    inverse = lax.rsqrt(squares / features + 1e-05)[:, None]
    normed = scaled * inverse * norm_gain[None, :]
    grad_scaled = (
        inverse * norm_gain[None, :] * out_grad
        - scaled * inverse * inverse * inverse * cross_terms[:, None] / features
    )
    grad_out = grad_scaled * head_scale[0]

    def backward_step(step_idx, state_pack):
        running, grad_q, grad_k, grad_v = state_pack
        block_idx = block_live - 1 - step_idx
        row_start = block_idx * GROUP
        q_block = lax.dynamic_slice_in_dim(q_rows, row_start, GROUP, 0)
        k_block = lax.dynamic_slice_in_dim(k_rows, row_start, GROUP, 0)
        v_block = lax.dynamic_slice_in_dim(v_rows, row_start, GROUP, 0)
        grad_block = lax.dynamic_slice_in_dim(grad_out, row_start, GROUP, 0)
        held_state = lax.dynamic_index_in_dim(saved_states, block_idx, 0, keepdims=False)
        scores = lax.dynamic_index_in_dim(saved_scores, block_idx, 0, keepdims=False)
        grad_vals = jnp.where(causal, plain_product(grad_block, v_block.T), 0.0)
        query_part = plain_product(grad_block, held_state.T) + plain_product(grad_vals, k_block)
        key_part = leading_product(grad_vals, q_block) + plain_product(v_block, running.T)
        value_part = leading_product(scores, grad_block) + plain_product(k_block, running)
        grad_q = lax.dynamic_update_slice_in_dim(grad_q, query_part, row_start, 0)
        grad_k = lax.dynamic_update_slice_in_dim(grad_k, key_part, row_start, 0)
        grad_v = lax.dynamic_update_slice_in_dim(grad_v, value_part, row_start, 0)
        running = running + leading_product(q_block, grad_block)
        return (running, grad_q, grad_k, grad_v)

    zero_rows = jnp.zeros((capacity, features_dev), jnp.float32)
    shard_grad, grad_q, grad_k, grad_v = lax.fori_loop(
        0, block_live, backward_step, (zero_state, zero_rows, zero_rows, zero_rows)
    )
    piece_rows = lax.all_gather(shard_grad[None], "seq", axis=0, tiled=True)
    picked = (jnp.arange(piece_rows.shape[0]) > shard_pos)[:, None, None]
    state_out = jnp.sum(jnp.where(picked, piece_rows, 0.0), axis=0)
    grad_query = jnp.where(live_rows, grad_q + plain_product(grad_out, state_in.T), 0.0)
    grad_key = jnp.where(live_rows, grad_k + plain_product(v_rows, state_out.T), 0.0)
    grad_value = jnp.where(live_rows, grad_v + plain_product(k_rows, state_out), 0.0)
    return (normed, grad_query, grad_key, grad_value)


def solution(mesh):
    in_specs = (
        P("seq", "head"),
        P("seq", "head"),
        P("seq", "head"),
        P("seq", "head"),
        P("head"),
        P("head"),
        P(),
    )
    out_specs = (P("seq", "head"), P("seq", "head"), P("seq", "head"), P("seq", "head"))
    return jax.shard_map(
        on_device, mesh=mesh, in_specs=in_specs, out_specs=out_specs, check_vma=False
    )
```

profile of v0, /device:TPU:0, one launch (start us, length us, event | category | flops | bytes accessed | tf_op | source)
XLA Modules:
  0.0 91.5 jit_solution(258238342465137067)
XLA Ops:
  0.6 0.0 copy-start
  0.6 0.0 copy-start.1
  0.7 1.2 %copy.12 = f32[768,128]{0,1:T(8,128)S(1)} copy(f32[768,128]{1,0:T(8,128)} %param.14) | data formatting | bytes 786432 | tf_op args[3]
  2.5 0.0 copy-start.6
  2.6 0.6 copy-done.6
  3.2 0.7 dynamic_slice.43
  4.6 0.0 copy-done
  4.6 0.0 copy-done.1
  4.6 1.2 %broadcast_select_fusion = (f32[768,128]{1,0:T(8,128)S(1)}, f32[768,128]{1,0:T(8,128)S(1)}, f32[768,128]{1,0:T(8,128)S(1)}) fusion(f32[768,128]{1,0:T(8,128)} %param.11, pred[768]{0:T(1024)(128)(4,1)S(1)} %iota_compare_fusion.2, f32[768,128]{1,0:T(8,128)S(1)} %copy-done, f32[768,128]{1,0:T(8,128)S(1)} %copy-done.1), kind=kLoop, calls=%fused_computation.68 | loop fusion | flops 294912 | bytes 2360064 | tf_op jit(solution)/shard_map/jit(_where)/select_n | solution.py:28
  5.9 4.4 %while.36 = (s32[]{:T(128)}, f32[128,128]{1,0:T(8,128)S(1)}, f32[768,128]{0,1:T(8,128)S(1)}, f32[6,128,128]{2,1,0:T(8,128)S(1)}, f32[6,128,128]{2,1,0:T(8,128)S(...) while((s32[]{:T(128)}, f32[128,128]{1,0:T(8,128)S(1)}, ...), condition=%wide.region_1.2_spmd.clone, body=%wide.region_0.1_spmd.clone.sunk | while | flops 100728832 | bytes 1379053 | solution.py:55
  6.6 0.2 fusion.94
  6.8 0.3 convolution_add_fusion.13
  7.1 0.3 bitcast_dynamic-update-slice_fusion.4
  7.4 0.2 convolution_add_fusion.14
  7.6 0.1 copy.24
  8.5 0.2 fusion.94
  8.7 0.3 convolution_add_fusion.13
  9.0 0.3 bitcast_dynamic-update-slice_fusion.4
  9.3 0.2 convolution_add_fusion.14
  9.5 0.1 copy.24
  10.3 0.0 copy-start.3
  10.3 0.0 copy-start.4
  10.3 20.9 %all-gather = f32[512,128]{1,0:T(8,128)S(1)} all-gather(f32[128,128]{1,0:T(8,128)S(1)} %get-tuple-element.221), channel_id=2, replica_groups=mesh['seq'=4,'head'=8] {'seq'}, dimensions={0}, use_global_device_ids=true | all-gather | bytes 327680 | tf_op jit(solution)/shard_map/all_gather | solution.py:58
  31.2 0.0 copy-done.3
  31.2 0.0 copy-start.5
  31.2 0.1 select_reduce_fusion.1
  31.3 0.6 copy-done.5
  31.9 0.6 multiply_reduce_fusion
  32.5 0.0 copy-done.4
  32.5 12.1 %all-reduce = (f32[768]{0:T(1024)S(1)}, f32[768]{0:T(1024)S(1)}) all-reduce(f32[768]{0:T(1024)S(1)} %get-tuple-element.296, f32[768]{0:T(1024)S(1)} %get-tuple-element.295), channel_id=1, replica_groups=mesh['seq'=4,'head'=8] {'head'}, use_global_device_ids=true, to_apply=%region_4.5 | all-reduce | flops 1536 | bytes 12288 | tf_op jit(solution)/shard_map/psum | solution.py:64
  44.6 0.1 subtract_multiply_fusion
  44.8 0.9 copy.15
  46.5 9.9 %while.37 = (s32[]{:T(128)}, f32[128,128]{1,0:T(8,128)S(1)}, f32[768,128]{1,0:T(8,128)S(1)}, f32[768,128]{1,0:T(8,128)S(1)}, f32[768,128]{1,0:T(8,128)S(1)}, /*i...) while((s32[]{:T(128)}, f32[128,128]{1,0:T(8,128)S(1)}, ...), condition=%wide.region_8.9_spmd.clone, body=%wide.region_7.8_spmd.clone.sunk | while | flops 201424896 | bytes 1840413 | solution.py:97
  47.2 1.1 %fusion.115 = f32[128,128]{1,0:T(8,128)S(1)} fusion(f32[6,128,128]{2,1,0:T(8,128)} %get-tuple-element.581, s32[]{:T(128)S(6)} %select_n.105, f32[768,128]{0,1:T(8,128)S(1)} %get-tuple-element.577, s32[]{:T(128)S(6)} %select_n.104), kind=kOutput, calls=%fused_computation.28.clone.1 | convolution fusion | flops 25165824 | bytes 196616 | tf_op jit(solution)/shard_map/while/body/dot_general | solution.py:14
  48.3 0.2 fusion.116
  48.6 0.3 convolution_select_fusion.3
  48.9 0.3 fusion.113
  49.2 0.3 fusion.114
  49.4 0.3 convolution_add_fusion.15
  49.7 1.1 %fusion.111 = f32[128,128]{1,0:T(8,128)S(1)} fusion(f32[6,128,128]{2,1,0:T(8,128)} %get-tuple-element.578, s32[]{:T(128)S(6)} %select_n.105, f32[768,128]{0,1:T(8,128)S(1)} %get-tuple-element.577, s32[]{:T(128)S(6)} %select_n.104), kind=kOutput, calls=%fused_computation.30.clone.1 | convolution fusion | flops 25165824 | bytes 196616 | tf_op jit(solution)/shard_map/while/body/dot_general | solution.py:10
  50.9 0.2 fusion.112
  51.8 1.1 %fusion.115 = f32[128,128]{1,0:T(8,128)S(1)} fusion(f32[6,128,128]{2,1,0:T(8,128)} %get-tuple-element.581, s32[]{:T(128)S(6)} %select_n.105, f32[768,128]{0,1:T(8,128)S(1)} %get-tuple-element.577, s32[]{:T(128)S(6)} %select_n.104), kind=kOutput, calls=%fused_computation.28.clone.1 | convolution fusion | flops 25165824 | bytes 196616 | tf_op jit(solution)/shard_map/while/body/dot_general | solution.py:14
  52.9 0.2 fusion.116
  53.2 0.3 convolution_select_fusion.3
  53.5 0.3 fusion.113
  53.8 0.3 fusion.114
  54.0 0.3 convolution_add_fusion.15
  54.3 1.1 %fusion.111 = f32[128,128]{1,0:T(8,128)S(1)} fusion(f32[6,128,128]{2,1,0:T(8,128)} %get-tuple-element.578, s32[]{:T(128)S(6)} %select_n.105, f32[768,128]{0,1:T(8,128)S(1)} %get-tuple-element.577, s32[]{:T(128)S(6)} %select_n.104), kind=kOutput, calls=%fused_computation.30.clone.1 | convolution fusion | flops 25165824 | bytes 196616 | tf_op jit(solution)/shard_map/while/body/dot_general | solution.py:10
  55.5 0.2 fusion.112
  56.4 1.5 %fusion.44 = f32[768,128]{1,0:T(8,128)} fusion(f32[768,128]{1,0:T(8,128)S(1)} %get-tuple-element.224, f32[768,128]{0,1:T(8,128)S(1)} %get-tuple-element.587, f32[128,128]{1,0:T(8,128)S(1)} %select_reduce_fusion.1, pred[768]{0:T(1024)(128)(4,1)S(1)} %iota_compare_fusion.2), kind=kOutput, calls=%fused_computation.59 | convolution fusion | flops 151191552 | bytes 1245952 | tf_op jit(solution)/shard_map/dot_general | solution.py:10
  57.9 30.9 %all-gather.1 = f32[512,128]{1,0:T(8,128)S(1)} all-gather(f32[128,128]{1,0:T(8,128)S(1)} %get-tuple-element.226), channel_id=3, replica_groups=mesh['seq'=4,'head'=8] {'seq'}, dimensions={0}, use_global_device_ids=true | all-gather | bytes 327680 | tf_op jit(solution)/shard_map/all_gather | solution.py:100
  88.8 0.1 select_reduce_fusion
  88.9 0.0 copy-start.2
  88.9 1.3 %fusion.45 = f32[768,128]{1,0:T(8,128)} fusion(f32[768,128]{1,0:T(8,128)S(1)} %get-tuple-element.225, f32[128,128]{1,0:T(8,128)S(1)} %select_reduce_fusion, pred[768]{0:T(1024)(128)(4,1)S(1)} %iota_compare_fusion.2, f32[768,128]{1,0:T(8,128)S(1)} %copy-done), kind=kOutput, calls=%fused_computation.60 | convolution fusion | flops 151289856 | bytes 1245952 | tf_op jit(solution)/shard_map/dot_general | solution.py:10
  90.2 0.0 copy-done.2
  90.2 1.3 %fusion.46 = f32[768,128]{1,0:T(8,128)} fusion(f32[768,128]{1,0:T(8,128)S(1)} %get-tuple-element.227, f32[128,128]{1,0:T(8,128)S(1)} %select_reduce_fusion, pred[768]{0:T(1024)(128)(4,1)S(1)} %iota_compare_fusion.2, f32[768,128]{1,0:T(8,128)S(1)} %copy-done.2), kind=kOutput, calls=%fused_computation.61 | convolution fusion | flops 151289856 | bytes 1245952 | tf_op jit(solution)/shard_map/dot_general | solution.py:10
  (16 shorter events, 0.2 us)
Async XLA Ops:
  0.6 3.9 %copy-start = (f32[768,128]{1,0:T(8,128)S(1)}, f32[768,128]{1,0:T(8,128)}, u32[]{:S(2)}) copy-start(f32[768,128]{1,0:T(8,128)} %param.13) | copy-start | bytes 1179652
  0.6 3.9 %copy-start.1 = (f32[768,128]{1,0:T(8,128)S(1)}, f32[768,128]{1,0:T(8,128)}, u32[]{:S(2)}) copy-start(f32[768,128]{1,0:T(8,128)} %param.12) | copy-start | bytes 1179652
  2.5 0.7 copy-start.6
  10.3 20.9 %copy-start.3 = (f32[6,128,128]{2,1,0:T(8,128)}, f32[6,128,128]{2,1,0:T(8,128)S(1)}, u32[]{:S(2)}) copy-start(f32[6,128,128]{2,1,0:T(8,128)S(1)} %get-tuple-element.542) | copy-start | bytes 1179652
  10.3 22.1 %copy-start.4 = (f32[6,128,128]{2,1,0:T(8,128)}, f32[6,128,128]{2,1,0:T(8,128)S(1)}, u32[]{:S(2)}) copy-start(f32[6,128,128]{2,1,0:T(8,128)S(1)} %get-tuple-element.545) | copy-start | bytes 1179652
  31.2 0.7 copy-start.5
  88.9 1.3 %copy-start.2 = (f32[768,128]{1,0:T(8,128)S(1)}, f32[768,128]{1,0:T(8,128)}, u32[]{:S(2)}) copy-start(f32[768,128]{1,0:T(8,128)} %param.12) | copy-start | bytes 1179652
where the time goes:
time: 92.4 us; the launch traced here: 91.5 us
  blocking collectives  63.9 us (69%)
  matrix products  14.3 us (15%)
  loops' own time  4.45 us (5%)
  local copies, waits for them, and re-layouts  4.44 us (5%)
  between operations  2.89 us (3%)
  other arithmetic  1.52 us (2%)
    all_gather x1, blocking collectives, on_device(): piece_rows = lax.all_gather(shard_grad[None], 'seq', axis=0, tiled=True)  30.9 us
    all_gather x1, blocking collectives, on_device(): piece_rows = lax.all_gather(shard_state[None], 'seq', axis=0, tiled=True)  20.9 us
    psum x1, blocking collectives, on_device(): lax.psum((jnp.sum(scaled * scaled, axis=1), jnp.sum(norm_gain[None, :] *...  12.1 us
    dot_general x20, matrix products, plain_product(): jnp.dot(left, right, precision=lax.Precision.HIGHEST, preferred_element_t...  10.3 us
    dot_general x8, matrix products, leading_product(): lax.dot_general(left, right, (((0,), (0,)), ((), ())), precision=lax.Prec...  4 us
    unnamed x16, local copies, waits for them, and re-layouts  3.38 us
    another operation x1, loops' own time, on_device(): lax.fori_loop(0, block_live, backward_step, (zero_state, zero_rows, zero_...  2.23 us
    another operation x1, loops' own time, on_device(): lax.fori_loop(0, block_live, forward_step, forward_init)  2.22 us

commit v1 on v0

--- a/solution.py
+++ b/solution.py
@@ -4,6 +4,19 @@
 from jax.sharding import PartitionSpec as P
 
 GROUP = 128
+
+
+def gather_around(x, axis, dim):
+    size, position, span = (lax.axis_size(axis), lax.axis_index(axis), x.shape[dim])
+    forward = [(i, (i + 1) % size) for i in range(size)]
+    result = jnp.zeros((*x.shape[:dim], size * span, *x.shape[dim + 1 :]), x.dtype)
+    carried = x
+    for hop in range(size):
+        source = (position - hop) % size
+        result = lax.dynamic_update_slice_in_dim(result, carried, source * span, axis=dim)
+        if hop < size - 1:
+            carried = lax.ppermute(carried, axis, forward)
+    return result
 
 
 def plain_product(left, right):
@@ -55,7 +68,7 @@
     shard_state, local_out, saved_states, saved_scores = lax.fori_loop(
         0, block_live, forward_step, forward_init
     )
-    piece_rows = lax.all_gather(shard_state[None], "seq", axis=0, tiled=True)
+    piece_rows = gather_around(shard_state[None], "seq", 0)
     picked = (jnp.arange(piece_rows.shape[0]) < shard_pos)[:, None, None]
     state_in = jnp.sum(jnp.where(picked, piece_rows, 0.0), axis=0)
     attended = local_out + plain_product(q_rows, state_in)

time: 92.4 us -> 84.4 us (0.913)
  blocking collectives: 63.9 us -> 36.2 us
  starting transfers between devices: 0 us -> 13.3 us
  waiting for transfers between devices: 0 us -> 9.51 us
  matrix products: 14.3 us -> 12.6 us
  local copies, waits for them, and re-layouts: 4.44 us -> 3.43 us
    all_gather x1 -> x0, blocking collectives: 20.9 us -> none  [on_device(): piece_rows = lax.all_gather(shard_state[None], 'seq', axis=0, tiled=True)]
    ppermute x0 -> x3, starting transfers between devices: none -> 13.3 us  [gather_around(): carried = lax.ppermute(carried, axis, forward)]
    ppermute x0 -> x3, waiting for transfers between devices: none -> 9.51 us  [gather_around(): carried = lax.ppermute(carried, axis, forward)]
    all_gather x1, blocking collectives: 30.9 us -> 24.1 us  [on_device(): piece_rows = lax.all_gather(shard_grad[None], 'seq', axis=0, tiled=True)]
    dot_general x20, matrix products: 10.3 us -> 8.62 us  [plain_product(): jnp.dot(left, right, precision=lax.Precision.HIGHEST, preferred_element_t...]
    unnamed x16 -> x14, local copies, waits for them, and re-layouts: 3.38 us -> 2.4 us
  transfers between devices with their start and end apart: 0 -> 3, of which waited for: 0 -> 3; matrix products, arithmetic and copies ran while one was open for 0% -> 0% of each run, Pallas kernels for 0% -> 0%
where the time goes in v1:
time: 84.4 us; the launch traced here: 83.8 us
  blocking collectives  36.2 us (43%)
  starting transfers between devices  13.3 us (16%)
  matrix products  12.6 us (15%)
  waiting for transfers between devices  9.51 us (11%)
  loops' own time  4.24 us (5%)
  local copies, waits for them, and re-layouts  3.43 us (4%)
  between operations  2.83 us (3%)
  other arithmetic  1.75 us (2%)
    all_gather x1, blocking collectives, on_device(): piece_rows = lax.all_gather(shard_grad[None], 'seq', axis=0, tiled=True)  24.1 us
    ppermute x3, starting transfers between devices, gather_around(): carried = lax.ppermute(carried, axis, forward)  13.3 us
    psum x1, blocking collectives, on_device(): lax.psum((jnp.sum(scaled * scaled, axis=1), jnp.sum(norm_gain[None, :] *...  12.1 us
    ppermute x3, waiting for transfers between devices, gather_around(): carried = lax.ppermute(carried, axis, forward)  9.51 us
    dot_general x20, matrix products, plain_product(): jnp.dot(left, right, precision=lax.Precision.HIGHEST, preferred_element_t...  8.62 us
    dot_general x8, matrix products, leading_product(): lax.dot_general(left, right, (((0,), (0,)), ((), ())), precision=lax.Prec...  4 us
    unnamed x14, local copies, waits for them, and re-layouts  2.4 us
    another operation x1, loops' own time, on_device(): lax.fori_loop(0, block_live, forward_step, forward_init)  2.14 us
  transfers between devices with their start and end apart: 3, of which 3 were waited for; matrix products, arithmetic and copies ran while one was open for 0% of the time, Pallas kernels for 0%

profile of v1, /device:TPU:0, one launch (start us, length us, event | category | flops | bytes accessed | tf_op | source)
XLA Modules:
  0.0 83.8 jit_solution(9700478550802493618)
XLA Ops:
  0.6 0.0 copy-start.5
  0.6 0.6 copy-done.5
  1.3 0.6 dynamic_slice.43
  2.5 1.4 %broadcast_select_fusion = (f32[768,128]{1,0:T(8,128)S(1)}, f32[768,128]{1,0:T(8,128)S(1)}, f32[768,128]{1,0:T(8,128)S(1)}) fusion(f32[768,128]{1,0:T(8,128)} %param.11, pred[768]{0:T(1024)(128)(4,1)S(1)} %iota_compare_fusion.2, f32[768,128]{1,0:T(8,128)} %param.13, f32[768,128]{1,0:T(8,128)} %param.12), kind=kLoop, calls=%fused_computation.68 | loop fusion | flops 294912 | bytes 2360064 | tf_op jit(solution)/shard_map/jit(_where)/select_n | solution.py:41
  4.1 0.0 copy-start.3
  4.1 4.3 %while.36 = (s32[]{:T(128)}, f32[128,128]{1,0:T(8,128)S(1)}, f32[768,128]{0,1:T(8,128)S(1)}, f32[6,128,128]{2,1,0:T(8,128)S(1)}, f32[6,128,128]{2,1,0:T(8,128)S(...) while((s32[]{:T(128)}, f32[128,128]{1,0:T(8,128)S(1)}, ...), condition=%wide.region_1.2_spmd.clone, body=%wide.region_0.1_spmd.clone.sunk | while | flops 100728832 | bytes 1379053 | solution.py:68
  4.8 0.2 fusion.94
  5.0 0.3 convolution_add_fusion.13
  5.3 0.3 bitcast_dynamic-update-slice_fusion.4
  5.6 0.2 convolution_add_fusion.14
  5.8 0.1 copy.24
  6.6 0.2 fusion.94
  6.8 0.3 convolution_add_fusion.13
  7.1 0.3 bitcast_dynamic-update-slice_fusion.4
  7.4 0.2 convolution_add_fusion.14
  7.6 0.1 copy.24
  8.4 0.0 copy-start.2
  8.4 10.4 %collective-permute-start = (f32[1,128,128]{2,1,0:T(8,128)S(1)}, f32[1,128,128]{2,1,0:T(8,128)S(1)}, u32[]{:S(2)}, u32[]{:S(2)}) collective-permute-start(f32[1,128,128]{2,1,0:T(8,128)S(1)} %bitcast.49), channel_id=1, source_target_pairs={{0,8},{8,16},{16,24},{24,0},{1,9},{9,17},{17,25},{25,1},{2,10},{10... | collective-permute-start | bytes 196616 | tf_op jit(solution)/shard_map/ppermute | solution.py:18
  18.8 0.0 copy-done.2
  19.4 0.0 copy-done.3
  19.4 0.2 copy.12
  20.4 0.3 collective-permute-done
  20.7 2.4 %collective-permute-start.1 = (f32[1,128,128]{2,1,0:T(8,128)S(1)}, f32[1,128,128]{2,1,0:T(8,128)S(1)}, u32[]{:S(2)}, u32[]{:S(2)}) collective-permute-start(f32[1,128,128]{2,1,0:T(8,128)S(1)} %collective-permute-done), channel_id=1, source_target_pairs={{0,8},{8,16},{16,24},{24,0},{1,9},{9,17},{17,25},{25,1},{2,10},{10... | collective-permute-start | bytes 196616 | tf_op jit(solution)/shard_map/ppermute | solution.py:18
  23.1 3.7 %collective-permute-done.1 = f32[1,128,128]{2,1,0:T(8,128)S(1)} collective-permute-done((f32[1,128,128]{2,1,0:T(8,128)S(1)}, f32[1,128,128]{2,1,0:T(8,128)S(1)}, u32[]{:S(2)}, u32[]{:S(2)}) %collective-permute-start.1) | collective-permute-done | bytes 65568 | tf_op jit(solution)/shard_map/ppermute | solution.py:18
  26.7 0.6 collective-permute-start.2
  27.3 5.5 %collective-permute-done.2 = f32[1,128,128]{2,1,0:T(8,128)S(1)} collective-permute-done((f32[1,128,128]{2,1,0:T(8,128)S(1)}, f32[1,128,128]{2,1,0:T(8,128)S(1)}, u32[]{:S(2)}, u32[]{:S(2)}) %collective-permute-start.2) | collective-permute-done | bytes 65568 | tf_op jit(solution)/shard_map/ppermute | solution.py:18
  32.8 0.1 select_reduce_fusion.1
  32.9 0.0 copy-start.4
  32.9 0.6 copy-done.4
  33.6 0.6 multiply_reduce_fusion
  34.2 12.1 %all-reduce = (f32[768]{0:T(1024)S(1)}, f32[768]{0:T(1024)S(1)}) all-reduce(f32[768]{0:T(1024)S(1)} %get-tuple-element.296, f32[768]{0:T(1024)S(1)} %get-tuple-element.295), channel_id=1, replica_groups=mesh['seq'=4,'head'=8] {'head'}, use_global_device_ids=true, to_apply=%region_4.5 | all-reduce | flops 1536 | bytes 12288 | tf_op jit(solution)/shard_map/psum | solution.py:77
  46.3 0.1 subtract_multiply_fusion
  46.5 0.9 %copy.15 = f32[768,128]{1,0:T(8,128)} copy(f32[768,128]{0,1:T(8,128)S(1)} %get-tuple-element.346) | data formatting | bytes 786432
  47.5 8.1 %while.37 = (s32[]{:T(128)}, f32[128,128]{1,0:T(8,128)S(1)}, f32[768,128]{1,0:T(8,128)S(1)}, f32[768,128]{1,0:T(8,128)S(1)}, f32[768,128]{1,0:T(8,128)S(1)}, /*i...) while((s32[]{:T(128)}, f32[128,128]{1,0:T(8,128)S(1)}, ...), condition=%wide.region_8.9_spmd.clone, body=%wide.region_7.8_spmd.clone.sunk | while | flops 201424896 | bytes 1840413 | solution.py:110
  48.2 1.1 %fusion.115 = f32[128,128]{1,0:T(8,128)S(1)} fusion(f32[6,128,128]{2,1,0:T(8,128)} %get-tuple-element.581, s32[]{:T(128)S(6)} %select_n.144, f32[768,128]{0,1:T(8,128)S(1)} %get-tuple-element.577, s32[]{:T(128)S(6)} %select_n.143), kind=kOutput, calls=%fused_computation.28.clone.1 | convolution fusion | flops 25165824 | bytes 196616 | tf_op jit(solution)/shard_map/while/body/dot_general | solution.py:27
  49.3 0.2 fusion.116
  49.5 0.3 convolution_select_fusion.3
  49.8 0.3 fusion.113
  50.1 0.3 fusion.114
  50.4 0.3 convolution_add_fusion.15
  50.7 0.3 fusion.111
  51.0 0.2 fusion.112
  51.9 1.1 %fusion.115 = f32[128,128]{1,0:T(8,128)S(1)} fusion(f32[6,128,128]{2,1,0:T(8,128)} %get-tuple-element.581, s32[]{:T(128)S(6)} %select_n.144, f32[768,128]{0,1:T(8,128)S(1)} %get-tuple-element.577, s32[]{:T(128)S(6)} %select_n.143), kind=kOutput, calls=%fused_computation.28.clone.1 | convolution fusion | flops 25165824 | bytes 196616 | tf_op jit(solution)/shard_map/while/body/dot_general | solution.py:27
  53.0 0.2 fusion.116
  53.2 0.3 convolution_select_fusion.3
  53.5 0.3 fusion.113
  53.8 0.3 fusion.114
  54.1 0.3 convolution_add_fusion.15
  54.4 0.3 fusion.111
  54.7 0.2 fusion.112
  55.6 1.5 %fusion.44 = f32[768,128]{1,0:T(8,128)} fusion(f32[768,128]{1,0:T(8,128)S(1)} %get-tuple-element.224, f32[768,128]{0,1:T(8,128)S(1)} %get-tuple-element.588, f32[128,128]{1,0:T(8,128)S(1)} %select_reduce_fusion.1, pred[768]{0:T(1024)(128)(4,1)S(1)} %iota_compare_fusion.2), kind=kOutput, calls=%fused_computation.59 | convolution fusion | flops 151191552 | bytes 1245952 | tf_op jit(solution)/shard_map/dot_general | solution.py:23
  57.1 0.0 copy-start
  57.1 24.1 %all-gather = f32[512,128]{1,0:T(8,128)S(1)} all-gather(f32[128,128]{1,0:T(8,128)S(1)} %get-tuple-element.226), channel_id=2, replica_groups=mesh['seq'=4,'head'=8] {'seq'}, dimensions={0}, use_global_device_ids=true | all-gather | bytes 327680 | tf_op jit(solution)/shard_map/all_gather | solution.py:113
  81.2 0.1 select_reduce_fusion
  81.3 0.0 copy-done
  81.3 0.0 copy-start.1
  81.3 1.3 %fusion.45 = f32[768,128]{1,0:T(8,128)} fusion(f32[768,128]{1,0:T(8,128)S(1)} %get-tuple-element.225, f32[128,128]{1,0:T(8,128)S(1)} %select_reduce_fusion, pred[768]{0:T(1024)(128)(4,1)S(1)} %iota_compare_fusion.2, f32[768,128]{1,0:T(8,128)S(1)} %copy-done), kind=kOutput, calls=%fused_computation.60 | convolution fusion | flops 151289856 | bytes 1245952 | tf_op jit(solution)/shard_map/dot_general | solution.py:23
  82.6 0.0 copy-done.1
  82.6 1.3 %fusion.46 = f32[768,128]{1,0:T(8,128)} fusion(f32[768,128]{1,0:T(8,128)S(1)} %get-tuple-element.227, f32[128,128]{1,0:T(8,128)S(1)} %select_reduce_fusion, pred[768]{0:T(1024)(128)(4,1)S(1)} %iota_compare_fusion.2, f32[768,128]{1,0:T(8,128)S(1)} %copy-done.1), kind=kOutput, calls=%fused_computation.61 | convolution fusion | flops 151289856 | bytes 1245952 | tf_op jit(solution)/shard_map/dot_general | solution.py:23
  (21 shorter events, 0.3 us)
Async XLA Ops:
  0.6 0.7 copy-start.5
  4.1 15.4 %copy-start.3 = (f32[768,128]{1,0:T(8,128)S(1)}, f32[768,128]{1,0:T(8,128)}, u32[]{:S(2)}) copy-start(f32[768,128]{1,0:T(8,128)} %param.14) | copy-start | bytes 1179652
  8.4 10.4 %copy-start.2 = (f32[6,128,128]{2,1,0:T(8,128)}, f32[6,128,128]{2,1,0:T(8,128)S(1)}, u32[]{:S(2)}) copy-start(f32[6,128,128]{2,1,0:T(8,128)S(1)} %get-tuple-element.545) | copy-start | bytes 1179652
  8.4 12.3 %collective-permute-start = (f32[1,128,128]{2,1,0:T(8,128)S(1)}, f32[1,128,128]{2,1,0:T(8,128)S(1)}, u32[]{:S(2)}, u32[]{:S(2)}) collective-permute-start(f32[1,128,128]{2,1,0:T(8,128)S(1)} %bitcast.49), channel_id=1, source_target_pairs={{0,8},{8,16},{16,24},{24,0},{1,9},{9,17},{17,25},{25,1},{2,10},{10... | collective-permute-start | bytes 196616 | tf_op jit(solution)/shard_map/ppermute | solution.py:18
  20.7 6.1 %collective-permute-start.1 = (f32[1,128,128]{2,1,0:T(8,128)S(1)}, f32[1,128,128]{2,1,0:T(8,128)S(1)}, u32[]{:S(2)}, u32[]{:S(2)}) collective-permute-start(f32[1,128,128]{2,1,0:T(8,128)S(1)} %collective-permute-done), channel_id=1, source_target_pairs={{0,8},{8,16},{16,24},{24,0},{1,9},{9,17},{17,25},{25,1},{2,10},{10... | collective-permute-start | bytes 196616 | tf_op jit(solution)/shard_map/ppermute | solution.py:18
  26.7 6.1 %collective-permute-start.2 = (f32[1,128,128]{2,1,0:T(8,128)S(1)}, f32[1,128,128]{2,1,0:T(8,128)S(1)}, u32[]{:S(2)}, u32[]{:S(2)}) collective-permute-start(f32[1,128,128]{2,1,0:T(8,128)S(1)} %collective-permute-done.1), channel_id=1, source_target_pairs={{0,8},{8,16},{16,24},{24,0},{1,9},{9,17},{17,25},{25,1},{2,10},{10... | collective-permute-start | bytes 196616 | tf_op jit(solution)/shard_map/ppermute | solution.py:18
  32.9 0.7 copy-start.4
  57.1 24.2 %copy-start = (f32[768,128]{1,0:T(8,128)S(1)}, f32[768,128]{1,0:T(8,128)}, u32[]{:S(2)}) copy-start(f32[768,128]{1,0:T(8,128)} %param.13) | copy-start | bytes 1179652
  81.3 1.3 %copy-start.1 = (f32[768,128]{1,0:T(8,128)S(1)}, f32[768,128]{1,0:T(8,128)}, u32[]{:S(2)}) copy-start(f32[768,128]{1,0:T(8,128)} %param.12) | copy-start | bytes 1179652
